TPU v7x, 32 devices: a whole 2x2x4 slice. The times are simulated.
32 devices in a mesh: dp: 4 (over z), seq: 8 (over y, x, core).
Axes of the slice: x: 2, y: 2, z: 4, core: 2. Of those that a mesh axis runs over, the one named last changes fastest.
Arguments:
- query_rows: bfloat16 [4, 3072, 1024], P('dp', 'seq'), may hold values from -48 to 48
- key_rows: bfloat16 [4, 3072, 1024], P('dp', 'seq'), may hold values from -8 to 8
- value_rows: bfloat16 [4, 3072, 1024], P('dp', 'seq'), may hold values from -6 to 6
- scale_end: int32 [3072], P('seq'), may hold values from 1 to 3072, as said below
- out_weight: bfloat16 [1024, 2048], replicated, may hold values from -0.8984375 to 0.8984375
- grad_out: bfloat16 [4, 3072, 2048], P('dp', 'seq'), may hold values from -1.5 to 1.5
Outputs:
- mixed_out: bfloat16 [4, 3072, 2048], P('dp', 'seq')
- out_grad: float32 [1024, 2048], P(('dp', 'seq'))
Inputs may be any that keep to these rules, and one draw needn't show every extreme that they name: scale_end is constant over each of 4 scales of consecutive tokens, equals the index one past the scale's last token (so scale_end[t] > t), never falls, and is 3072 on the last scale; the same for every image.
All inputs are finite; a program needn't handle non-finite values.
Results may differ from a plain program's by a relative error of at most 0.014.
Values may be sent and summed in bfloat16 or wider, within the bound.
No kernel may reach another device: no remote copies, remote signals or barrier semaphores. Data moves between devices by JAX's collectives and lax.ppermute only.
A program may use at most 256 MiB of HBM per device.

v0:
```python
import jax
import jax.numpy as jnp
from jax import lax
from jax.sharding import PartitionSpec as P

HEAD = 128
floor_score = -1e30


def attend_piece(carry, queries, query_end, key_piece, value_piece):
    run_max, run_sum, weighted = carry
    key_count = key_piece.shape[0]
    scores = jnp.einsum(
        "qge,kge->qgk", queries, key_piece, preferred_element_type=jnp.float32
    ) * queries.shape[2] ** (-0.5)
    positions = jnp.arange(key_count, dtype=jnp.int32)
    visible = (positions[None, :] < query_end[:, None])[:, None, :]
    masked = jnp.where(visible, scores, floor_score)
    new_max = jnp.maximum(run_max, jnp.max(masked, axis=2))
    weights = jnp.where(visible, jnp.exp(masked - new_max[:, :, None]), 0.0)
    run_sum = jnp.sum(weights, axis=2)
    product = jnp.einsum(
        "qgk,kge->qge",
        weights.astype(jnp.bfloat16),
        value_piece,
        preferred_element_type=jnp.float32,
    )
    weighted = product
    return (new_max, run_sum, weighted)


def guarded(carry, queries, query_end, key_piece, value_piece, offset):
    reach_end = jnp.max(query_end)

    def compute(state):
        return attend_piece(state, queries, query_end, key_piece, value_piece)

    def unchanged(state):
        return state

    return lax.cond(offset < reach_end, compute, unchanged, carry)


def initial_state(query_count, head_count):
    return (
        jnp.full((query_count, head_count), floor_score, jnp.float32),
        jnp.zeros((query_count, head_count), jnp.float32),
        jnp.zeros((query_count, head_count, HEAD), jnp.float32),
    )


def body(query_rows, key_rows, value_rows, scale_end, out_weight, grad_out):
    row_count = query_rows.shape[1]
    full_width = query_rows.shape[2]
    head_count = full_width // HEAD
    local_q = query_rows[0].reshape(row_count, head_count, HEAD)
    key_piece = lax.all_gather(key_rows[0], "seq", axis=0, tiled=True)
    value_piece = lax.all_gather(value_rows[0], "seq", axis=0, tiled=True)
    key_count = key_piece.shape[0]
    run_max, run_sum, weighted = guarded(
        initial_state(row_count, head_count),
        local_q,
        scale_end,
        key_piece.reshape(key_count, head_count, HEAD),
        value_piece.reshape(key_count, head_count, HEAD),
        jnp.int32(0),
    )
    attended = (weighted / run_sum[:, :, None]).astype(jnp.bfloat16).reshape(row_count, full_width)
    mixed_out = jnp.dot(attended, out_weight, preferred_element_type=jnp.float32).astype(
        jnp.bfloat16
    )[None]
    local_grad = grad_out[0]
    shares = lax.psum_scatter(
        lax.dot_general(
            attended, local_grad, (((0,), (0,)), ((), ())), preferred_element_type=jnp.float32
        ).astype(jnp.bfloat16),
        "dp",
        scatter_dimension=0,
        tiled=True,
    )
    grad_shard = lax.psum_scatter(shares, "seq", scatter_dimension=0, tiled=True).astype(
        jnp.float32
    )
    return (mixed_out, grad_shard)


def solution(mesh):
    placed = (
        P("dp", "seq", None),
        P("dp", "seq", None),
        P("dp", "seq", None),
        P("seq"),
        P(),
        P("dp", "seq", None),
    )
    return jax.shard_map(
        body,
        mesh=mesh,
        in_specs=placed,
        out_specs=(P("dp", "seq", None), P(("dp", "seq"), None)),
        check_vma=False,
    )
```

profile of v0, /device:TPU:0, one launch (start us, length us, event | category | flops | bytes accessed | tf_op | source)
XLA Modules:
  0.0 295.5 jit_solution(3256707269969613751)
XLA Ops:
  7.2 0.0 all-gather.5.cloned.1.call-start
  7.2 0.7 all-gather.5.cloned.1.call-update
  7.9 0.0 all-gather.7.cloned.1.call-start
  8.0 0.7 all-gather.7.cloned.1.call-update
  8.7 0.0 reduce-scatter.3.cloned.1.call-start
  8.7 1.3 reduce_max.18
  10.7 47.3 %all-gather.5.cloned.1.call-done = bf16[1,3072,1024]{2,1,0:T(8,128)(2,1)} async-done(((bf16[1,384,1024]{2,1,0:T(8,128)(2,1)}), bf16[1,3072,1024]{2,1,0:T(8,128)(2,1)}) %all-gather.5.cloned.1.call-update) | async-done | bytes 6291472 | tf_op jit(solution)/shard_map/all_gather | solution.py:57
  58.0 47.3 %all-gather.7.cloned.1.call-done = bf16[1,3072,1024]{2,1,0:T(8,128)(2,1)} async-done(((bf16[1,384,1024]{2,1,0:T(8,128)(2,1)}), bf16[1,3072,1024]{2,1,0:T(8,128)(2,1)}) %all-gather.7.cloned.1.call-update) | async-done | bytes 6291472 | tf_op jit(solution)/shard_map/all_gather | solution.py:58
  105.3 60.2 %conditional.1 = (f32[384,8]{0,1:T(8,128)S(1)}, f32[384,8,128]{0,2,1:T(8,128)S(1)}) conditional(s32[]{:T(128)} %convert_element_type.18, () %tuple.16, (s32[384]{0:T(512)}, bf16[3072,1024]{1,0:T(8,128)(2,1)}, bf16[1,384,1024]{2,1,0:T(8,128)(2,1)}, bf16[3072,1024]{1,0:T(8,128)(2,1)}) %tuple.33), branch_computations={%region_1.0_spmd, %region_2.5_spmd} | conditional | flops 4955698176 | bytes 137700880 | solution.py:41
  105.3 1.3 copy.30
  106.6 1.6 iota_compare_fusion
  108.2 17.6 %fusion = (f32[384,8]{0,1:T(8,128)S(1)}, f32[8,3072,384]{2,1,0:T(8,128)}) fusion(pred[384,3072]{0,1:T(8,128)(4,1)S(1)} %iota_compare_fusion, bf16[384,8,128]{2,1,0:T(8,128)(2,1)S(1)} %bitcast.48, bf16[3072,1024]{1,0:T(8,128)(2,1)} %get-tuple-element.12), kind=kOutput, calls=%fused_computation.2 | convolution fusion | flops 2444227584 | bytes 46018560 | tf_op jit(solution)/shard_map/cond/branch_1_fun/qge,kge->qgk/dot_general | solution.py:13
  125.8 21.0 %fusion.11 = f32[384,8,128]{2,0,1:T(8,128)} fusion(f32[8,3072,384]{2,1,0:T(8,128)} %get-tuple-element.25, f32[384,8]{0,1:T(8,128)S(1)} %broadcast_maximum_fusion, pred[384,3072]{0,1:T(8,128)(4,1)S(1)} %iota_compare_fusion, bf16[3072,1024]{1,0:T(8,128)(2,1)} %get-tuple-element.14), kind=kOutput, calls=%fused_computation.13 | convolution fusion | flops 2463105024 | bytes 46804992 | tf_op jit(solution)/shard_map/cond/branch_1_fun/qgk,kge->qge/dot_general | solution.py:22
  146.8 16.6 %fusion.2 = f32[384,8]{0,1:T(8,128)S(1)} fusion(f32[8,3072,384]{2,1,0:T(8,128)} %get-tuple-element.25, f32[384,8]{0,1:T(8,128)S(1)} %broadcast_maximum_fusion, pred[384,3072]{0,1:T(8,128)(4,1)S(1)} %iota_compare_fusion), kind=kLoop, calls=%fused_computation.4 | loop fusion | flops 47182848 | bytes 38952960 | tf_op jit(solution)/shard_map/cond/branch_1_fun/reduce_sum | solution.py:21
  163.4 1.9 copy.27
  165.5 0.1 divide_convert_fusion
  165.7 0.9 copy-done.1
  166.6 4.3 %convolution_convert_fusion = bf16[1024,2048]{1,0:T(8,128)(2,1)} fusion(bf16[384,1024]{0,1:T(8,128)(2,1)S(1)} %bitcast.49, bf16[1,384,2048]{2,1,0:T(8,128)(2,1)S(1)} %copy-done), kind=kOutput, calls=%fused_computation.19 | convolution fusion | flops 1612709888 | bytes 6553600 | tf_op jit(solution)/shard_map/dot_general | solution.py:74
  170.9 0.0 reduce-scatter.3.cloned.1.call-update
  170.9 0.0 reduce-scatter.5.cloned.1.call-start
  170.9 76.9 %reduce-scatter.3.cloned.1.call-done = bf16[256,2048]{1,0:T(8,128)(2,1)} async-done(((bf16[1024,2048]{1,0:T(8,128)(2,1)}), bf16[256,2048]{1,0:T(8,128)(2,1)}) %reduce-scatter.3.cloned.1.call-update) | async-done | bytes 1048592 | tf_op jit(solution)/shard_map/reduce_scatter | solution.py:73
  247.8 5.4 %fusion.20 = bf16[1,384,2048]{2,1,0:T(8,128)(2,1)} fusion(bf16[384,1024]{0,1:T(8,128)(2,1)} %bitcast.50, bf16[1024,2048]{1,0:T(8,128)(2,1)} %param.12), kind=kOutput, calls=%fused_computation.21 | convolution fusion | flops 1611399168 | bytes 6553600 | tf_op jit(solution)/shard_map/dot_general | solution.py:69
  253.2 34.1 %reduce-scatter.5.cloned.1.call-done = bf16[32,2048]{1,0:T(8,128)(2,1)} async-done(((bf16[256,2048]{1,0:T(8,128)(2,1)}), bf16[32,2048]{1,0:T(8,128)(2,1)}) %reduce-scatter.5.cloned.1.call-update) | async-done | bytes 131088 | tf_op jit(solution)/shard_map/reduce_scatter | solution.py:81
  287.3 1.6 convert_element_type.22
  (5 shorter events, 0.0 us)
Async XLA Ops:
  7.2 159.4 %copy-start = (bf16[1,384,2048]{2,1,0:T(8,128)(2,1)S(1)}, bf16[1,384,2048]{2,1,0:T(8,128)(2,1)}, u32[]{:S(2)}) copy-start(bf16[1,384,2048]{2,1,0:T(8,128)(2,1)} %param.13) | copy-start | bytes 4718596
  7.2 50.8 %all-gather.5.cloned.1.call-start = ((), (), s32[]{:S(2)}) async-start(), calls=%async_computation.4 | async-start | bytes 7077888 | tf_op jit(solution)/shard_map/all_gather | solution.py:57
  7.9 97.4 %all-gather.7.cloned.1.call-start = ((), (), s32[]{:S(2)}) async-start(), calls=%async_computation.5 | async-start | bytes 7077888 | tf_op jit(solution)/shard_map/all_gather | solution.py:58
  8.7 239.1 %reduce-scatter.3.cloned.1.call-start = ((), (), s32[]{:S(2)}) async-start(), calls=%async_computation.2 | async-start | bytes 5242880 | tf_op jit(solution)/shard_map/reduce_scatter | solution.py:73
  165.6 0.9 copy-start.1
  170.9 116.5 %reduce-scatter.5.cloned.1.call-start = ((), (), s32[]{:S(2)}) async-start(), calls=%async_computation.3 | async-start | bytes 1179648 | tf_op jit(solution)/shard_map/reduce_scatter | solution.py:81
Sparse Core Ops, SparseCore 0:
  9.9 48.1 all-gather.4
  59.9 45.3 all-gather.6
  171.0 76.7 reduce-scatter.2
  250.8 36.4 reduce-scatter.4
where the time goes:
time: 296 us; the launch traced here: 295 us
  waiting for transfers between devices  207 us (70%)
  matrix products  48.3 us (16%)
  other arithmetic  21.3 us (7%)
  between operations  14.4 us (5%)
  local copies, waits for them, and re-layouts  4.09 us (1%)
    reduce_scatter x1, waiting for transfers between devices, body(): lax.psum_scatter(lax.dot_general(attended, local_grad, (((0,), (0,)), (()...  76.9 us
    all_gather x1, waiting for transfers between devices, body(): key_piece = lax.all_gather(key_rows[0], 'seq', axis=0, tiled=True)  47.3 us
    all_gather x1, waiting for transfers between devices, body(): value_piece = lax.all_gather(value_rows[0], 'seq', axis=0, tiled=True)  47.3 us
    reduce_scatter x1, waiting for transfers between devices, body(): lax.psum_scatter(shares, 'seq', scatter_dimension=0, tiled=True)  34.1 us
    dot_general x1, matrix products, attend_piece(): jnp.einsum('qgk,kge->qge', weights.astype(jnp.bfloat16), value_piece, pre...  21 us
    dot_general x1, matrix products, attend_piece(): jnp.einsum('qge,kge->qgk', queries, key_piece, preferred_element_type=jnp...  17.6 us
    reduce_sum x1, other arithmetic, attend_piece(): run_sum = jnp.sum(weights, axis=2)  16.6 us
  transfers between devices with their start and end apart: 4, of which 4 were waited for; matrix products, arithmetic and copies ran while one was open for 2% of the time, Pallas kernels for 0%

commit v1 on v0

--- a/solution.py
+++ b/solution.py
@@ -55,7 +55,12 @@
     head_count = full_width // HEAD
     local_q = query_rows[0].reshape(row_count, head_count, HEAD)
     key_piece = lax.all_gather(key_rows[0], "seq", axis=0, tiled=True)
-    value_piece = lax.all_gather(value_rows[0], "seq", axis=0, tiled=True)
+    ring = [value_rows[0]]
+    for hop in range(7):
+        ring.append(lax.ppermute(ring[-1], "seq", [(dev, (dev + 1) % 8) for dev in range(8)]))
+    value_piece = jnp.roll(
+        jnp.concatenate(ring[::-1], axis=0), (lax.axis_index("seq") + 1) * ring[0].shape[0], axis=0
+    )
     key_count = key_piece.shape[0]
     run_max, run_sum, weighted = guarded(
         initial_state(row_count, head_count),

time: 296 us -> 344 us (1.16)
  local copies, waits for them, and re-layouts: 4.09 us -> 43.3 us
  waiting for transfers between devices: 207 us -> 215 us
    ppermute x0 -> x7, waiting for transfers between devices: none -> 104 us  [body(): lax.ppermute(ring[-1], 'seq', [(dev, (dev + 1) % 8) for dev in range(8)])]
    all_gather x1, waiting for transfers between devices: 47.3 us -> 0.01 us  [body(): key_piece = lax.all_gather(key_rows[0], 'seq', axis=0, tiled=True)]
    all_gather x1 -> x0, waiting for transfers between devices: 47.3 us -> none  [body(): value_piece = lax.all_gather(value_rows[0], 'seq', axis=0, tiled=True)]
    unnamed x4 -> x38, local copies, waits for them, and re-layouts: 0.92 us -> 30.5 us
    dynamic_slice x0 -> x1, local copies, waits for them, and re-layouts: none -> 8.57 us  [body(): jnp.roll(jnp.concatenate(ring[::-1], axis=0), (lax.axis_index('seq') + 1)...]
  transfers between devices with their start and end apart: 4 -> 10, of which waited for: 4 -> 9; matrix products, arithmetic and copies ran while one was open for 2% -> 10% of each run, Pallas kernels for 0% -> 0%
where the time goes in v1:
time: 344 us; the launch traced here: 343 us
  waiting for transfers between devices  215 us (62%)
  matrix products  48 us (14%)
  local copies, waits for them, and re-layouts  43.3 us (13%)
  other arithmetic  20.6 us (6%)
  between operations  14.5 us (4%)
    ppermute x7, waiting for transfers between devices, body(): lax.ppermute(ring[-1], 'seq', [(dev, (dev + 1) % 8) for dev in range(8)])  104 us
    reduce_scatter x1, waiting for transfers between devices, body(): lax.psum_scatter(lax.dot_general(attended, local_grad, (((0,), (0,)), (()...  76 us
    reduce_scatter x1, waiting for transfers between devices, body(): lax.psum_scatter(shares, 'seq', scatter_dimension=0, tiled=True)  34.3 us
    unnamed x38, local copies, waits for them, and re-layouts  30.5 us
    dot_general x1, matrix products, attend_piece(): jnp.einsum('qgk,kge->qge', weights.astype(jnp.bfloat16), value_piece, pre...  20.6 us
    dot_general x1, matrix products, attend_piece(): jnp.einsum('qge,kge->qgk', queries, key_piece, preferred_element_type=jnp...  17.7 us
    reduce_sum x1, other arithmetic, attend_piece(): run_sum = jnp.sum(weights, axis=2)  16.6 us
    dynamic_slice x1, local copies, waits for them, and re-layouts, body(): jnp.roll(jnp.concatenate(ring[::-1], axis=0), (lax.axis_index('seq') + 1)...  8.57 us
  transfers between devices with their start and end apart: 10, of which 9 were waited for; matrix products, arithmetic and copies ran while one was open for 10% of the time, Pallas kernels for 0%

profile of v1, /device:TPU:0, one launch (start us, length us, event | category | flops | bytes accessed | tf_op | source)
XLA Modules:
  0.0 342.9 jit_solution(13746021363013871691)
XLA Ops:
  10.0 12.5 %collective-permute-done = bf16[384,1024]{0,1:T(8,128)(2,1)S(1)} collective-permute-done((bf16[384,1024]{0,1:T(8,128)(2,1)S(1)}, bf16[384,1024]{0,1:T(8,128)(2,1)S(1)}, u32[]{:S(2)}, u32[]{:S(2)}) %collective-permute-start) | collective-permute-done | bytes 786464 | tf_op jit(solution)/shard_map/ppermute | solution.py:60
  22.8 17.9 %collective-permute-done.1 = bf16[384,1024]{0,1:T(8,128)(2,1)S(1)} collective-permute-done((bf16[384,1024]{0,1:T(8,128)(2,1)S(1)}, bf16[384,1024]{0,1:T(8,128)(2,1)S(1)}, u32[]{:S(2)}, u32[]{:S(2)}) %collective-permute-start.1) | collective-permute-done | bytes 786464 | tf_op jit(solution)/shard_map/ppermute | solution.py:60
  41.6 26.3 %collective-permute-done.2 = bf16[384,1024]{0,1:T(8,128)(2,1)S(1)} collective-permute-done((bf16[384,1024]{0,1:T(8,128)(2,1)S(1)}, bf16[384,1024]{0,1:T(8,128)(2,1)S(1)}, u32[]{:S(2)}, u32[]{:S(2)}) %collective-permute-start.2) | collective-permute-done | bytes 786464 | tf_op jit(solution)/shard_map/ppermute | solution.py:60
  68.9 12.3 %collective-permute-done.3 = bf16[384,1024]{0,1:T(8,128)(2,1)S(1)} collective-permute-done((bf16[384,1024]{0,1:T(8,128)(2,1)S(1)}, bf16[384,1024]{0,1:T(8,128)(2,1)S(1)}, u32[]{:S(2)}, u32[]{:S(2)}) %collective-permute-start.3) | collective-permute-done | bytes 786464 | tf_op jit(solution)/shard_map/ppermute | solution.py:60
  82.1 12.3 %collective-permute-done.4 = bf16[384,1024]{0,1:T(8,128)(2,1)S(1)} collective-permute-done((bf16[384,1024]{0,1:T(8,128)(2,1)S(1)}, bf16[384,1024]{0,1:T(8,128)(2,1)S(1)}, u32[]{:S(2)}, u32[]{:S(2)}) %collective-permute-start.4) | collective-permute-done | bytes 786464 | tf_op jit(solution)/shard_map/ppermute | solution.py:60
  95.2 12.4 %collective-permute-done.5 = bf16[384,1024]{0,1:T(8,128)(2,1)} collective-permute-done((bf16[384,1024]{0,1:T(8,128)(2,1)S(1)}, bf16[384,1024]{0,1:T(8,128)(2,1)}, u32[]{:S(2)}, u32[]{:S(2)}) %collective-permute-start.5) | collective-permute-done | bytes 786464 | tf_op jit(solution)/shard_map/ppermute | solution.py:60
  109.7 10.6 %collective-permute-done.6 = bf16[384,1024]{0,1:T(8,128)(2,1)} collective-permute-done((bf16[384,1024]{0,1:T(8,128)(2,1)}, bf16[384,1024]{0,1:T(8,128)(2,1)}, u32[]{:S(2)}, u32[]{:S(2)}) %collective-permute-start.6) | collective-permute-done | bytes 786464 | tf_op jit(solution)/shard_map/ppermute | solution.py:60
  120.3 2.1 constant_dynamic-update-slice_fusion.15
  122.4 2.1 constant_dynamic-update-slice_fusion.14
  124.5 2.1 constant_dynamic-update-slice_fusion.13
  126.7 2.2 constant_dynamic-update-slice_fusion.12
  128.8 2.2 constant_dynamic-update-slice_fusion.11
  131.0 2.1 constant_dynamic-update-slice_fusion.10
  135.2 2.2 constant_dynamic-update-slice_fusion.7
  137.4 2.2 constant_dynamic-update-slice_fusion.6
  145.8 67.8 %conditional.1 = (f32[384,8]{0,1:T(8,128)S(1)}, f32[384,8,128]{0,2,1:T(8,128)S(1)}) conditional(s32[]{:T(128)} %convert_element_type.21, () %tuple.28, (s32[384]{0:T(512)S(1)}, bf16[3072,1024]{1,0:T(8,128)(2,1)}, bf16[1,384,1024]{2,1,0:T(8,128)(2,1)}, s32[]{:T(128)}, bf16[6144,1024]{0,1:T(8,128)(2,1)}) %tuple.43), branch_computations={%region_1.2_spmd, %region_2.5_spmd} | conditional | flops 4955698176 | bytes 150283936 | solution.py:41
  148.1 8.6 %constant_dynamic-slice_fusion = bf16[3072,1024]{0,1:T(8,128)(2,1)} fusion(bf16[6144,1024]{0,1:T(8,128)(2,1)} %get-tuple-element.100, s32[]{:T(128)S(6)} %select_n.32), kind=kLoop, calls=%fused_computation.14 | loop fusion | bytes 12582916 | tf_op jit(solution)/shard_map/jit(_roll_dynamic)/dynamic_slice | solution.py:61
  156.6 17.7 %fusion = (f32[384,8]{0,1:T(8,128)S(1)}, f32[8,3072,384]{2,1,0:T(8,128)}) fusion(pred[384,3072]{0,1:T(8,128)(4,1)S(1)} %iota_compare_fusion, bf16[384,8,128]{2,1,0:T(8,128)(2,1)S(1)} %bitcast.45, bf16[3072,1024]{1,0:T(8,128)(2,1)} %get-tuple-element.98), kind=kOutput, calls=%fused_computation.2 | convolution fusion | flops 2444227584 | bytes 46018560 | tf_op jit(solution)/shard_map/cond/branch_1_fun/qge,kge->qgk/dot_general | solution.py:13
  174.3 20.6 %fusion.9 = f32[384,8,128]{2,0,1:T(8,128)} fusion(bf16[3072,8,128]{0,2,1:T(8,128)(2,1)} %bitcast.43, f32[8,3072,384]{2,1,0:T(8,128)} %get-tuple-element.112, f32[384,8]{0,1:T(8,128)S(1)} %broadcast_maximum_fusion, pred[384,3072]{0,1:T(8,128)(4,1)S(1)} %iota_compare_fusion), kind=kOutput, calls=%fused_computation.11 | convolution fusion | flops 2463105024 | bytes 46804992 | tf_op jit(solution)/shard_map/cond/branch_1_fun/qgk,kge->qge/dot_general | solution.py:22
  194.9 16.6 %fusion.2 = f32[384,8]{0,1:T(8,128)S(1)} fusion(f32[8,3072,384]{2,1,0:T(8,128)} %get-tuple-element.112, f32[384,8]{0,1:T(8,128)S(1)} %broadcast_maximum_fusion, pred[384,3072]{0,1:T(8,128)(4,1)S(1)} %iota_compare_fusion), kind=kLoop, calls=%fused_computation.4 | loop fusion | flops 47182848 | bytes 38952960 | tf_op jit(solution)/shard_map/cond/branch_1_fun/reduce_sum | solution.py:21
  214.7 4.3 %convolution_convert_fusion = bf16[1024,2048]{1,0:T(8,128)(2,1)} fusion(bf16[384,1024]{0,1:T(8,128)(2,1)S(1)} %bitcast.46, bf16[1,384,2048]{2,1,0:T(8,128)(2,1)S(1)} %copy-done), kind=kOutput, calls=%fused_computation.18 | convolution fusion | flops 1612709888 | bytes 6553600 | tf_op jit(solution)/shard_map/dot_general | solution.py:79
  219.1 76.0 %reduce-scatter.3.cloned.1.call-done = bf16[256,2048]{1,0:T(8,128)(2,1)} async-done(((bf16[1024,2048]{1,0:T(8,128)(2,1)}), bf16[256,2048]{1,0:T(8,128)(2,1)}) %reduce-scatter.3.cloned.1.call-update) | async-done | bytes 1048592 | tf_op jit(solution)/shard_map/reduce_scatter | solution.py:78
  295.1 5.4 %fusion.16 = bf16[1,384,2048]{2,1,0:T(8,128)(2,1)} fusion(bf16[384,1024]{0,1:T(8,128)(2,1)} %bitcast.47, bf16[1024,2048]{1,0:T(8,128)(2,1)} %param.12), kind=kOutput, calls=%fused_computation.20 | convolution fusion | flops 1611399168 | bytes 6553600 | tf_op jit(solution)/shard_map/dot_general | solution.py:74
  300.5 34.3 %reduce-scatter.5.cloned.1.call-done = bf16[32,2048]{1,0:T(8,128)(2,1)} async-done(((bf16[256,2048]{1,0:T(8,128)(2,1)}), bf16[32,2048]{1,0:T(8,128)(2,1)}) %reduce-scatter.5.cloned.1.call-update) | async-done | bytes 131088 | tf_op jit(solution)/shard_map/reduce_scatter | solution.py:86
  (52 shorter events, 23.2 us)
Async XLA Ops:
  7.2 207.6 %copy-start = (bf16[1,384,2048]{2,1,0:T(8,128)(2,1)S(1)}, bf16[1,384,2048]{2,1,0:T(8,128)(2,1)}, u32[]{:S(2)}) copy-start(bf16[1,384,2048]{2,1,0:T(8,128)(2,1)} %param.13) | copy-start | bytes 4718596
  7.2 138.7 %all-gather.3.cloned.1.call-start = ((), (), s32[]{:S(2)}) async-start(), calls=%async_computation.4 | async-start | bytes 7077888 | tf_op jit(solution)/shard_map/all_gather | solution.py:57
  7.9 287.2 %reduce-scatter.3.cloned.1.call-start = ((), (), s32[]{:S(2)}) async-start(), calls=%async_computation.2 | async-start | bytes 5242880 | tf_op jit(solution)/shard_map/reduce_scatter | solution.py:78
  9.5 13.1 %collective-permute-start = (bf16[384,1024]{0,1:T(8,128)(2,1)S(1)}, bf16[384,1024]{0,1:T(8,128)(2,1)S(1)}, u32[]{:S(2)}, u32[]{:S(2)}) collective-permute-start(bf16[384,1024]{0,1:T(8,128)(2,1)S(1)} %bitcast.42), channel_id=1, source_target_pairs={{0,1},{1,2},{2,3},{3,4},{4,5},{5,6},{6,7},{7,0},{8,9},{9,10},{10,1... | collective-permute-start | bytes 2359304 | tf_op jit(solution)/shard_map/ppermute | solution.py:60
  22.5 18.1 %collective-permute-start.1 = (bf16[384,1024]{0,1:T(8,128)(2,1)S(1)}, bf16[384,1024]{0,1:T(8,128)(2,1)S(1)}, u32[]{:S(2)}, u32[]{:S(2)}) collective-permute-start(bf16[384,1024]{0,1:T(8,128)(2,1)S(1)} %collective-permute-done), channel_id=1, source_target_pairs={{0,1},{1,2},{2,3},{3,4},{4,5},{5,6},{6,7},{7,0},{8,9},{9,10},{10,1... | collective-permute-start | bytes 2359304 | tf_op jit(solution)/shard_map/ppermute | solution.py:60
  40.7 0.9 copy-start.1
  41.6 26.3 %collective-permute-start.2 = (bf16[384,1024]{0,1:T(8,128)(2,1)S(1)}, bf16[384,1024]{0,1:T(8,128)(2,1)S(1)}, u32[]{:S(2)}, u32[]{:S(2)}) collective-permute-start(bf16[384,1024]{0,1:T(8,128)(2,1)S(1)} %collective-permute-done.1), channel_id=1, source_target_pairs={{0,1},{1,2},{2,3},{3,4},{4,5},{5,6},{6,7},{7,0},{8,9},{9,10},{10,1... | collective-permute-start | bytes 2359304 | tf_op jit(solution)/shard_map/ppermute | solution.py:60
  67.9 0.9 copy-start.3
  68.8 12.3 %collective-permute-start.3 = (bf16[384,1024]{0,1:T(8,128)(2,1)S(1)}, bf16[384,1024]{0,1:T(8,128)(2,1)S(1)}, u32[]{:S(2)}, u32[]{:S(2)}) collective-permute-start(bf16[384,1024]{0,1:T(8,128)(2,1)S(1)} %collective-permute-done.2), channel_id=1, source_target_pairs={{0,1},{1,2},{2,3},{3,4},{4,5},{5,6},{6,7},{7,0},{8,9},{9,10},{10,1... | collective-permute-start | bytes 2359304 | tf_op jit(solution)/shard_map/ppermute | solution.py:60
  81.2 0.9 copy-start.5
  82.0 12.3 %collective-permute-start.4 = (bf16[384,1024]{0,1:T(8,128)(2,1)S(1)}, bf16[384,1024]{0,1:T(8,128)(2,1)S(1)}, u32[]{:S(2)}, u32[]{:S(2)}) collective-permute-start(bf16[384,1024]{0,1:T(8,128)(2,1)S(1)} %collective-permute-done.3), channel_id=1, source_target_pairs={{0,1},{1,2},{2,3},{3,4},{4,5},{5,6},{6,7},{7,0},{8,9},{9,10},{10,1... | collective-permute-start | bytes 2359304 | tf_op jit(solution)/shard_map/ppermute | solution.py:60
  94.4 0.9 copy-start.7
  95.2 12.4 %collective-permute-start.5 = (bf16[384,1024]{0,1:T(8,128)(2,1)S(1)}, bf16[384,1024]{0,1:T(8,128)(2,1)}, u32[]{:S(2)}, u32[]{:S(2)}) collective-permute-start(bf16[384,1024]{0,1:T(8,128)(2,1)S(1)} %collective-permute-done.4), channel_id=1, source_target_pairs={{0,1},{1,2},{2,3},{3,4},{4,5},{5,6},{6,7},{7,0},{8,9},{9,10},{10,1... | collective-permute-start | bytes 2359304 | tf_op jit(solution)/shard_map/ppermute | solution.py:60
  107.7 12.6 %collective-permute-start.6 = (bf16[384,1024]{0,1:T(8,128)(2,1)}, bf16[384,1024]{0,1:T(8,128)(2,1)}, u32[]{:S(2)}, u32[]{:S(2)}) collective-permute-start(bf16[384,1024]{0,1:T(8,128)(2,1)} %collective-permute-done.5), channel_id=1, source_target_pairs={{0,1},{1,2},{2,3},{3,4},{4,5},{5,6},{6,7},{7,0},{8,9},{9,10},{10,1... | collective-permute-start | bytes 2359304 | tf_op jit(solution)/shard_map/ppermute | solution.py:60
  109.6 29.9 %copy-start.8 = (bf16[384,1024]{0,1:T(8,128)(2,1)S(1)}, bf16[384,1024]{0,1:T(8,128)(2,1)}, u32[]{:S(2)}) copy-start(bf16[384,1024]{0,1:T(8,128)(2,1)} %copy-done.7) | copy-start | bytes 2359300
  109.7 31.0 %copy-start.6 = (bf16[384,1024]{0,1:T(8,128)(2,1)S(1)}, bf16[384,1024]{0,1:T(8,128)(2,1)}, u32[]{:S(2)}) copy-start(bf16[384,1024]{0,1:T(8,128)(2,1)} %copy-done.5) | copy-start | bytes 2359300
  109.7 32.0 %copy-start.4 = (bf16[384,1024]{0,1:T(8,128)(2,1)S(1)}, bf16[384,1024]{0,1:T(8,128)(2,1)}, u32[]{:S(2)}) copy-start(bf16[384,1024]{0,1:T(8,128)(2,1)} %copy-done.3) | copy-start | bytes 2359300
  109.7 33.0 %copy-start.2 = (bf16[384,1024]{0,1:T(8,128)(2,1)S(1)}, bf16[384,1024]{0,1:T(8,128)(2,1)}, u32[]{:S(2)}) copy-start(bf16[384,1024]{0,1:T(8,128)(2,1)} %copy-done.1) | copy-start | bytes 2359300
  109.7 36.2 %copy-start.10 = (s32[384]{0:T(512)S(1)}, s32[384]{0:T(512)}, u32[]{:S(2)}) copy-start(s32[384]{0:T(512)} %param.11) | copy-start | bytes 4612
  213.8 0.9 copy-start.9
  219.0 115.7 %reduce-scatter.5.cloned.1.call-start = ((), (), s32[]{:S(2)}) async-start(), calls=%async_computation.3 | async-start | bytes 1179648 | tf_op jit(solution)/shard_map/reduce_scatter | solution.py:86
Sparse Core Ops, SparseCore 0:
  9.9 57.1 all-gather.2
  219.2 75.8 reduce-scatter.2
  298.3 36.4 reduce-scatter.4
